TPU v7x, 256 devices: a whole 4x4x8 slice. The times are simulated.
256 devices in a mesh: space: 32 (over z, x), sample: 8 (over y, core).
Axes of the slice: x: 4, y: 4, z: 8, core: 2. Of those that a mesh axis runs over, the one named last changes fastest.
Arguments:
- crops: bfloat16 [256, 16, 64, 1024], P('sample', None, 'space'), may hold values from -6 to 6
- first_kernel: bfloat16 [32, 16, 3, 3, 3], replicated, may hold values from -0.3125 to 0.3125
- second_kernel: bfloat16 [64, 32, 3, 3, 3], replicated, may hold values from -0.21875 to 0.21875
- out_grad: bfloat16 [256, 64, 16, 64], P(('sample', 'space')), may hold values from -0.03125 to 0.03125
Outputs:
- features_out: bfloat16 [256, 64, 16, 64], P(('sample', 'space'))
- first_grad: float32 [32, 16, 3, 3, 3], replicated
- second_grad: float32 [64, 32, 3, 3, 3], replicated
All inputs are finite; a program needn't handle non-finite values.
Results may differ from a plain program's by a relative error of at most 0.012.
Values may be sent and summed in bfloat16 or wider, within the bound.
A program may use at most 128 MiB of HBM per device.

v0:
```python
import jax
import jax.numpy as jnp
from jax import lax
from jax.sharding import PartitionSpec as P

HEIGHT = 8
WIDTH = 128


def forward_conv(field, kernel, depth_pad):
    return lax.conv_general_dilated(
        field,
        kernel,
        (2, 2, 2),
        (depth_pad, (1, 0), (1, 0)),
        dimension_numbers=("NCDHW", "OIDHW", "NCDHW"),
        preferred_element_type=jnp.float32,
    )


def kernel_grad(field, cotangent, depth_pad):
    return lax.conv_general_dilated(
        field,
        cotangent,
        (1, 1, 1),
        (depth_pad, (1, 0), (1, 0)),
        rhs_dilation=(2, 2, 2),
        dimension_numbers=("CNDHW", "IODHW", "CNDHW"),
        preferred_element_type=jnp.float32,
    )


def input_grad(cotangent, kernel):
    flipped = kernel[:, :, ::-1, ::-1, ::-1]
    return lax.conv_general_dilated(
        cotangent,
        flipped,
        (1, 1, 1),
        ((1, 2), (1, 2), (1, 2)),
        lhs_dilation=(2, 2, 2),
        dimension_numbers=("NCDHW", "IODHW", "NCDHW"),
        preferred_element_type=jnp.float32,
    )


def silu_slope(value):
    sigma = jax.nn.sigmoid(value)
    return sigma * (1.0 + value * (1.0 - sigma))


def body(crops, first_kernel, second_kernel, out_grad):
    local_samples, channels_in, planes, flat_cells = crops.shape
    whole_input = lax.all_to_all(crops, "space", split_axis=0, concat_axis=2, tiled=True)
    whole_input = whole_input.reshape(
        whole_input.shape[0], channels_in, whole_input.shape[2], HEIGHT, WIDTH
    )
    first_pre = forward_conv(whole_input, first_kernel, (1, 0))
    act_whole = jax.nn.silu(first_pre).astype(jnp.bfloat16)
    sample_count = act_whole.shape[0]
    second_pre = forward_conv(act_whole, second_kernel, (1, 0))
    features_out = second_pre.astype(jnp.bfloat16).reshape(out_grad.shape)
    cotangent = out_grad.reshape(
        sample_count, out_grad.shape[1], out_grad.shape[2], HEIGHT // 4, WIDTH // 4
    )
    second_grad = kernel_grad(act_whole, cotangent, (1, 0))
    act_grad = input_grad(cotangent, second_kernel).astype(jnp.bfloat16)
    pre_grad = (act_grad.astype(jnp.float32) * silu_slope(first_pre)).astype(jnp.bfloat16)
    first_grad = kernel_grad(whole_input, pre_grad, (1, 0))
    first_grad, second_grad = lax.psum((first_grad, second_grad), ("space", "sample"))
    return (features_out, first_grad, second_grad)


def solution(mesh):
    placed = (P("sample", None, "space", None), P(), P(), P(("sample", "space"), None, None, None))
    return jax.shard_map(
        body,
        mesh=mesh,
        in_specs=placed,
        out_specs=(P(("sample", "space"), None, None, None), P(), P()),
        check_vma=False,
    )
```

profile of v0, /device:TPU:1, one launch (start us, length us, event | category | flops | bytes accessed | tf_op | source)
XLA Modules:
  0.0 415.9 jit_solution(15933746394667295038)
XLA Ops:
  7.2 12.0 %all-to-all-start = ((bf16[32,16,2,1024]{3,2,1,0:T(2,128)(2,1)}), bf16[32,16,2,1024]{3,2,1,0:T(2,128)(2,1)S(1)}, u32[]{:S(2)}, u32[]{:S(2)}) async-start(bf16[32,16,2,1024]{3,2,1,0:T(2,128)(2,1)} %param.4), calls=%async_computation | async-start | bytes 4194304 | tf_op jit(solution)/shard_map/all_to_all | solution.py:53
  19.3 1.2 copy.72
  20.5 0.2 copy.91
  20.9 2.4 fusion.19
  23.3 5.4 %copy.76 = f32[32,4,8,10,32]{4,0,3,2,1:T(8,128)} copy(f32[32,4,8,10,32]{4,2,3,1,0:T(8,128)S(1)} %fusion.19) | data formatting | bytes 2621440 | tf_op jit(solution)/shard_map/convert_element_type | solution.py:67
  28.7 39.0 %all-to-all-done = bf16[32,16,2,1024]{3,2,1,0:T(2,128)(2,1)S(1)} async-done(((bf16[32,16,2,1024]{3,2,1,0:T(2,128)(2,1)}), bf16[32,16,2,1024]{3,2,1,0:T(2,128)(2,1)S(1)}, u32[]{:S(2)}, u32[]{:S(2)}) %all-to-all-start) | async-done | bytes 2097184 | tf_op jit(solution)/shard_map/all_to_all | solution.py:53
  67.7 0.7 copy.60
  68.4 0.6 copy.92
  69.0 5.3 %copy.90 = bf16[16,64,8,1,128]{1,2,4,0,3:T(8,128)(2,1)} copy(bf16[16,64,8,1,128]{4,2,0,1,3:T(8,128)(2,1)S(1)} %bitcast.48) | data formatting | bytes 4194304
  74.3 5.6 %pad.clone = bf16[16,64,8,1,144]{1,2,4,0,3:T(8,128)(2,1)} pad(bf16[16,64,8,1,128]{1,2,4,0,3:T(8,128)(2,1)} %copy.90, bf16[]{:T(256)} %constant.6), padding=0_0x0_0x0_0x0_0x1_15 | pad | bytes 4456450 | tf_op jit(solution)/shard_map/reshape | solution.py:54
  79.9 32.5 %copy.63 = bf16[16,64,8,1,8,18]{0,4,5,2,1,3:T(8,128)(2,1)} copy(bf16[16,64,8,1,8,18]{1,2,5,4,0,3:T(8,128)(2,1)} %bitcast.50) | data formatting | bytes 4718592 | tf_op jit(solution)/shard_map/conv_general_dilated | solution.py:11
  112.4 3.9 slice.9
  116.3 20.1 %broadcast_select_fusion = (bf16[32,4,8,9,32]{4,2,3,1,0:T(8,128)(2,1)}, bf16[32,4,8,9,32]{4,2,3,1,0:T(8,128)(2,1)}, f32[32,4,8,9,32]{4,2,3,1,0:T(8,128)}) fusion(pred[8,9]{0,1:T(8,128)(4,1)S(1)} %copy-done.7, bf16[32,16,3,3,3]{0,1,4,3,2:T(8,128)(2,1)S(1)} %copy-done.8, bf16[16,64,8,1,7,2]{0,4,5,2,1,3:T(8,128)(2,1)} %slice.9, ...), kind=kOutput, calls=%fused_computation.30 | convolution fusion | flops 241065984 | bytes 4975688 | tf_op jit(solution)/shard_map/conv_general_dilated | solution.py:11
  136.4 2.6 copy.64
  139.0 0.4 slice.10
  139.4 1.4 copy.66
  140.8 1.0 fusion.48
  141.8 0.4 copy-done.1
  142.3 0.9 copy.80
  143.2 1.7 slice.16
  144.9 12.4 %fusion.9 = f32[64,32,3,3,3]{0,1,4,3,2:T(8,128)} fusion(bf16[32,4,1,64,32]{4,0,3,1,2:T(8,128)(2,1)} %slice.16, bf16[1,64,16,2,32]{1,4,3,2,0:T(8,128)(2,1)S(1)} %bitcast.60), kind=kOutput, calls=%fused_computation.16 | convolution fusion | flops 91443200 | bytes 876544 | tf_op jit(solution)/shard_map/conv_general_dilated | solution.py:22
  157.3 3.9 add_multiply_fusion
  161.2 4.9 %copy.77 = f32[32,4,8,9,32]{4,0,3,2,1:T(8,128)} copy(f32[32,4,8,9,32]{4,2,3,1,0:T(8,128)S(1)} %add_multiply_fusion) | data formatting | bytes 2359296 | tf_op jit(solution)/shard_map/mul | solution.py:48
  166.1 35.1 %copy.78 = bf16[1,16,64,8,128]{1,0,4,3,2:T(2,128)(2,1)} copy(bf16[1,16,64,8,128]{4,3,1,2,0:T(8,128)(2,1)S(1)} %bitcast.49) | data formatting | bytes 4194304 | tf_op jit(solution)/shard_map/reshape | solution.py:54
  201.2 4.5 %fusion.8 = bf16[32,4,1,64,32]{4,0,3,1,2:T(8,128)(2,1)S(1)} fusion(f32[32,4,1,72,32]{4,0,3,1,2:T(8,128)} %bitcast.52, f32[32,4,1,80,32]{4,0,3,1,2:T(8,128)} %bitcast.51), kind=kLoop, calls=%fused_computation.15 | loop fusion | flops 524288 | bytes 2621440 | tf_op jit(solution)/shard_map/convert_element_type | solution.py:67
  205.7 89.5 %fusion.11 = f32[32,16,3,3,3]{0,1,4,3,2:T(8,128)S(1)} fusion(bf16[1,16,64,8,128]{1,0,4,3,2:T(2,128)(2,1)} %copy.78, bf16[32,4,1,64,32]{4,0,3,1,2:T(8,128)(2,1)S(1)} %fusion.8), kind=kOutput, calls=%fused_computation.18 | convolution fusion | flops 204385280 | bytes 2676736 | tf_op jit(solution)/shard_map/conv_general_dilated | solution.py:22
  295.3 1.8 fusion.26
  297.1 0.2 copy.69
  297.3 1.1 copy.84
  298.4 79.8 %psum.14 = f32[32,16,3,3,3]{0,1,4,3,2:T(8,128)} all-reduce(f32[32,16,3,3,3]{0,1,4,3,2:T(8,128)S(1)} %fusion.11), channel_id=1, replica_groups=mesh['space'=32,'sample'=8] {'space','sample'}, use_global_device_ids=true, to_apply=%region_0.1 | all-reduce | flops 13824 | bytes 110592 | tf_op jit(solution)/shard_map/psum | solution.py:69
  378.2 28.8 %all-reduce.2.cloned.1.call-done = f32[64,32,3,3,3]{0,1,4,3,2:T(8,128)} async-done(((f32[64,32,3,3,3]{0,1,4,3,2:T(8,128)}), f32[64,32,3,3,3]{0,1,4,3,2:T(8,128)}) %all-reduce.2.cloned.1.call-update) | async-done | bytes 221200 | tf_op jit(solution)/shard_map/psum | solution.py:69
  407.0 1.8 copy.101
  (22 shorter events, 0.3 us)
Async XLA Ops:
  7.2 13.7 %copy-start = (bf16[64,32,3,3,3]{0,1,4,3,2:T(8,128)(2,1)S(1)}, bf16[64,32,3,3,3]{0,1,4,3,2:T(8,128)(2,1)}, u32[]{:S(2)}) copy-start(bf16[64,32,3,3,3]{0,1,4,3,2:T(8,128)(2,1)} %param.6) | copy-start | bytes 331780
  7.2 13.7 %copy-start.6 = (pred[8,10]{0,1:T(8,128)(4,1)S(1)}, pred[8,10]{0,1:T(8,128)(4,1)}, u32[]{:S(2)}) copy-start(pred[8,10]{0,1:T(8,128)(4,1)} %constant.19) | copy-start | bytes 244
  7.2 60.5 %all-to-all-start = ((bf16[32,16,2,1024]{3,2,1,0:T(2,128)(2,1)}), bf16[32,16,2,1024]{3,2,1,0:T(2,128)(2,1)S(1)}, u32[]{:S(2)}, u32[]{:S(2)}) async-start(bf16[32,16,2,1024]{3,2,1,0:T(2,128)(2,1)} %param.4), calls=%async_computation | async-start | bytes 4194304 | tf_op jit(solution)/shard_map/all_to_all | solution.py:53
  19.2 387.8 %all-reduce.2.cloned.1.call-start = ((), (), s32[]{:S(2)}) async-start(), calls=%async_computation.1 | async-start | bytes 884736 | tf_op jit(solution)/shard_map/psum | solution.py:69
  79.9 36.3 %copy-start.7 = (pred[8,9]{0,1:T(8,128)(4,1)S(1)}, pred[8,9]{0,1:T(8,128)(4,1)}, u32[]{:S(2)}) copy-start(pred[8,9]{0,1:T(8,128)(4,1)} %constant.17) | copy-start | bytes 220
  79.9 36.3 %copy-start.8 = (bf16[32,16,3,3,3]{0,1,4,3,2:T(8,128)(2,1)S(1)}, bf16[32,16,3,3,3]{0,1,4,3,2:T(8,128)(2,1)}, u32[]{:S(2)}) copy-start(bf16[32,16,3,3,3]{0,1,4,3,2:T(8,128)(2,1)} %param.5) | copy-start | bytes 82948
  139.0 3.3 copy-start.3
  140.8 1.5 copy-start.1
  205.7 89.6 %copy-start.2 = (bf16[32,4,1,8,8,32]{5,3,4,1,0,2:T(8,128)(2,1)S(1)}, bf16[32,4,1,8,8,32]{5,3,4,1,0,2:T(8,128)(2,1)}, u32[]{:S(2)}) copy-start(bf16[32,4,1,8,8,32]{5,3,4,1,0,2:T(8,128)(2,1)} %copy-done.1) | copy-start | bytes 1572868
  205.7 89.6 %copy-start.4 = (bf16[32,4,1,7,1,32]{5,3,4,1,0,2:T(8,128)(2,1)S(1)}, bf16[32,4,1,7,1,32]{5,3,4,1,0,2:T(8,128)(2,1)}, u32[]{:S(2)}) copy-start(bf16[32,4,1,7,1,32]{5,3,4,1,0,2:T(8,128)(2,1)} %get-tuple-element.14) | copy-start | bytes 172036
  205.7 89.6 %copy-start.5 = (bf16[32,4,1,7,1,32]{5,3,4,1,0,2:T(8,128)(2,1)S(1)}, bf16[32,4,1,7,1,32]{5,3,4,1,0,2:T(8,128)(2,1)}, u32[]{:S(2)}) copy-start(bf16[32,4,1,7,1,32]{5,3,4,1,0,2:T(8,128)(2,1)} %get-tuple-element.15) | copy-start | bytes 172036
Sparse Core Ops, SparseCore 0:
  157.4 249.5 all-reduce.1
where the time goes:
time: 422 us; the launch traced here: 416 us
  matrix products  126 us (30%)
  local copies, waits for them, and re-layouts  107 us (25%)
  blocking collectives  79.8 us (19%)
  waiting for transfers between devices  67.7 us (16%)
  between operations  14.5 us (3%)
  starting transfers between devices  12 us (3%)
  other arithmetic  8.48 us (2%)
    conv_general_dilated x2, matrix products, kernel_grad(): lax.conv_general_dilated(field, cotangent, (1, 1, 1), (depth_pad, (1, 0),...  102 us
    psum x1, blocking collectives, body(): lax.psum((first_grad, second_grad), ('space', 'sample'))  79.8 us
    reshape x2, local copies, waits for them, and re-layouts, body(): whole_input.reshape(whole_input.shape[0], channels_in, whole_input.shape[...  40.7 us
    all_to_all x1, waiting for transfers between devices, body(): lax.all_to_all(crops, 'space', split_axis=0, concat_axis=2, tiled=True)  39 us
    conv_general_dilated x2, local copies, waits for them, and re-layouts, forward_conv(): lax.conv_general_dilated(field, kernel, (2, 2, 2), (depth_pad, (1, 0), (1...  36.3 us
    psum x1, waiting for transfers between devices, body(): lax.psum((first_grad, second_grad), ('space', 'sample'))  28.8 us
    conv_general_dilated x2, matrix products, forward_conv(): lax.conv_general_dilated(field, kernel, (2, 2, 2), (depth_pad, (1, 0), (1...  22 us
    all_to_all x1, starting transfers between devices, body(): lax.all_to_all(crops, 'space', split_axis=0, concat_axis=2, tiled=True)  12 us
  transfers between devices with their start and end apart: 2, of which 2 were waited for; matrix products, arithmetic and copies ran while one was open for 36% of the time, Pallas kernels for 0%

commit v1 on v0

--- a/solution.py
+++ b/solution.py
@@ -1,3 +1,4 @@
+import functools
 import jax
 import jax.numpy as jnp
 from jax import lax
@@ -5,6 +6,15 @@
 
 HEIGHT = 8
 WIDTH = 128
+
+
+def handle_circles(point, axis_tag, axis_id):
+    last = lax.psum(point, axis_tag)
+    v_next = lax.psum(last, axis_id)
+    return v_next
+
+
+edit_edges = functools.partial(handle_circles, axis_tag="sample", axis_id="space")
 
 
 def forward_conv(field, kernel, depth_pad):
@@ -66,7 +76,7 @@
     act_grad = input_grad(cotangent, second_kernel).astype(jnp.bfloat16)
     pre_grad = (act_grad.astype(jnp.float32) * silu_slope(first_pre)).astype(jnp.bfloat16)
     first_grad = kernel_grad(whole_input, pre_grad, (1, 0))
-    first_grad, second_grad = lax.psum((first_grad, second_grad), ("space", "sample"))
+    first_grad, second_grad = edit_edges((first_grad, second_grad))
     return (features_out, first_grad, second_grad)
 
 

time: 422 us -> 480 us (1.14)
  the two profiles are of different devices: /device:TPU:1 before, /device:TPU:0 now
where the time goes in v1:
time: 480 us; the launch traced here: 473 us
  blocking collectives  169 us (35%)
  matrix products  125 us (26%)
  local copies, waits for them, and re-layouts  105 us (22%)
  waiting for transfers between devices  40.7 us (8%)
  between operations  14.5 us (3%)
  starting transfers between devices  9.81 us (2%)
  other arithmetic  8.46 us (2%)
    psum x1, blocking collectives, handle_circles(): v_next = lax.psum(last, axis_id)  143 us
    conv_general_dilated x2, matrix products, kernel_grad(): lax.conv_general_dilated(field, cotangent, (1, 1, 1), (depth_pad, (1, 0),...  101 us
    all_to_all x1, waiting for transfers between devices, body(): lax.all_to_all(crops, 'space', split_axis=0, concat_axis=2, tiled=True)  40.6 us
    reshape x2, local copies, waits for them, and re-layouts, body(): whole_input.reshape(whole_input.shape[0], channels_in, whole_input.shape[...  40.4 us
    conv_general_dilated x2, local copies, waits for them, and re-layouts, forward_conv(): lax.conv_general_dilated(field, kernel, (2, 2, 2), (depth_pad, (1, 0), (1...  36.3 us
    psum x1, blocking collectives, handle_circles(): last = lax.psum(point, axis_tag)  26.4 us
    conv_general_dilated x2, matrix products, forward_conv(): lax.conv_general_dilated(field, kernel, (2, 2, 2), (depth_pad, (1, 0), (1...  22 us
    unnamed x18, local copies, waits for them, and re-layouts  10.2 us
  transfers between devices with their start and end apart: 3, of which 1 were waited for; matrix products, arithmetic and copies ran while one was open for 32% of the time, Pallas kernels for 0%

profile of v1, /device:TPU:0, one launch (start us, length us, event | category | flops | bytes accessed | tf_op | source)
XLA Modules:
  0.0 473.4 jit_solution(460807770984108524)
XLA Ops:
  7.2 9.7 %all-to-all-start = ((bf16[32,16,2,1024]{3,2,1,0:T(2,128)(2,1)}), bf16[32,16,2,1024]{3,2,1,0:T(2,128)(2,1)S(1)}, u32[]{:S(2)}, u32[]{:S(2)}) async-start(bf16[32,16,2,1024]{3,2,1,0:T(2,128)(2,1)} %param.4), calls=%async_computation | async-start | bytes 4194304 | tf_op jit(solution)/shard_map/all_to_all | solution.py:63
  17.0 1.2 copy.72
  18.2 0.2 copy.91
  18.4 0.1 copy.75
  18.6 2.4 fusion.19
  21.0 5.4 %copy.76 = f32[32,4,8,10,32]{4,0,3,2,1:T(8,128)} copy(f32[32,4,8,10,32]{4,2,3,1,0:T(8,128)S(1)} %fusion.19) | data formatting | bytes 2621440 | tf_op jit(solution)/shard_map/convert_element_type | solution.py:77
  26.4 40.6 %all-to-all-done = bf16[32,16,2,1024]{3,2,1,0:T(2,128)(2,1)S(1)} async-done(((bf16[32,16,2,1024]{3,2,1,0:T(2,128)(2,1)}), bf16[32,16,2,1024]{3,2,1,0:T(2,128)(2,1)S(1)}, u32[]{:S(2)}, u32[]{:S(2)}) %all-to-all-start) | async-done | bytes 2097184 | tf_op jit(solution)/shard_map/all_to_all | solution.py:63
  67.1 0.7 copy.60
  67.8 0.6 copy.92
  68.4 5.3 %copy.90 = bf16[16,64,8,1,128]{1,2,4,0,3:T(8,128)(2,1)} copy(bf16[16,64,8,1,128]{4,2,0,1,3:T(8,128)(2,1)S(1)} %bitcast.48) | data formatting | bytes 4194304
  73.7 5.6 %pad.clone = bf16[16,64,8,1,144]{1,2,4,0,3:T(8,128)(2,1)} pad(bf16[16,64,8,1,128]{1,2,4,0,3:T(8,128)(2,1)} %copy.90, bf16[]{:T(256)} %constant.6), padding=0_0x0_0x0_0x0_0x1_15 | pad | bytes 4456450 | tf_op jit(solution)/shard_map/reshape | solution.py:64
  79.3 32.5 %copy.63 = bf16[16,64,8,1,8,18]{0,4,5,2,1,3:T(8,128)(2,1)} copy(bf16[16,64,8,1,8,18]{1,2,5,4,0,3:T(8,128)(2,1)} %bitcast.50) | data formatting | bytes 4718592 | tf_op jit(solution)/shard_map/conv_general_dilated | solution.py:21
  111.7 3.8 slice.9
  115.6 20.2 %broadcast_select_fusion = (bf16[32,4,8,9,32]{4,2,3,1,0:T(8,128)(2,1)}, bf16[32,4,8,9,32]{4,2,3,1,0:T(8,128)(2,1)}, f32[32,4,8,9,32]{4,2,3,1,0:T(8,128)}) fusion(pred[8,9]{0,1:T(8,128)(4,1)S(1)} %copy-done.4, bf16[32,16,3,3,3]{0,1,4,3,2:T(8,128)(2,1)S(1)} %copy-done.5, bf16[16,64,8,1,7,2]{0,4,5,2,1,3:T(8,128)(2,1)} %slice.9, ...), kind=kOutput, calls=%fused_computation.30 | convolution fusion | flops 241065984 | bytes 4975688 | tf_op jit(solution)/shard_map/conv_general_dilated | solution.py:21
  135.7 2.6 copy.64
  138.3 0.4 slice.10
  138.8 2.6 copy.66
  141.4 0.9 copy.80
  142.3 0.4 slice.16
  142.7 11.8 %fusion.9 = f32[64,32,3,3,3]{0,1,4,3,2:T(8,128)} fusion(bf16[32,4,1,64,32]{4,0,3,1,2:T(8,128)(2,1)S(1)} %slice.16, bf16[1,64,16,2,32]{1,4,3,2,0:T(8,128)(2,1)S(1)} %bitcast.60), kind=kOutput, calls=%fused_computation.16 | convolution fusion | flops 91443200 | bytes 876544 | tf_op jit(solution)/shard_map/conv_general_dilated | solution.py:32
  154.6 3.9 add_multiply_fusion
  158.5 4.9 %copy.77 = f32[32,4,8,9,32]{4,0,3,2,1:T(8,128)} copy(f32[32,4,8,9,32]{4,2,3,1,0:T(8,128)S(1)} %add_multiply_fusion) | data formatting | bytes 2359296 | tf_op jit(solution)/shard_map/mul | solution.py:58
  163.4 34.8 %copy.78 = bf16[1,16,64,8,128]{1,0,4,3,2:T(2,128)(2,1)} copy(bf16[1,16,64,8,128]{4,3,1,2,0:T(8,128)(2,1)S(1)} %bitcast.49) | data formatting | bytes 4194304 | tf_op jit(solution)/shard_map/reshape | solution.py:64
  198.2 4.5 fusion.8
  202.8 89.3 %fusion.11 = f32[32,16,3,3,3]{0,1,4,3,2:T(8,128)S(1)} fusion(bf16[1,16,64,8,128]{1,0,4,3,2:T(2,128)(2,1)} %copy.78, bf16[32,4,1,64,32]{4,0,3,1,2:T(8,128)(2,1)S(1)} %fusion.8), kind=kOutput, calls=%fused_computation.18 | convolution fusion | flops 204385280 | bytes 2676736 | tf_op jit(solution)/shard_map/conv_general_dilated | solution.py:32
  292.0 0.1 fusion.48
  292.2 1.8 fusion.26
  294.0 0.2 copy.69
  294.2 1.1 copy.84
  295.3 26.4 %psum.28 = f32[32,16,3,3,3]{0,1,4,3,2:T(8,128)S(1)} all-reduce(f32[32,16,3,3,3]{0,1,4,3,2:T(8,128)S(1)} %fusion.11), channel_id=1, replica_groups=mesh['space'=32,'sample'=8] {'sample'}, use_global_device_ids=true, to_apply=%region_0.1 | all-reduce | flops 13824 | bytes 110592 | tf_op jit(solution)/shard_map/psum | solution.py:12
  321.7 142.8 %psum.29 = f32[32,16,3,3,3]{0,1,4,3,2:T(8,128)} all-reduce(f32[32,16,3,3,3]{0,1,4,3,2:T(8,128)S(1)} %psum.28), channel_id=1, replica_groups=mesh['space'=32,'sample'=8] {'space'}, use_global_device_ids=true, to_apply=%region_1.2 | all-reduce | flops 13824 | bytes 110592 | tf_op jit(solution)/shard_map/psum | solution.py:13
  464.6 1.8 copy.102
  (20 shorter events, 0.2 us)
Async XLA Ops:
  7.2 11.4 %copy-start = (bf16[64,32,3,3,3]{0,1,4,3,2:T(8,128)(2,1)S(1)}, bf16[64,32,3,3,3]{0,1,4,3,2:T(8,128)(2,1)}, u32[]{:S(2)}) copy-start(bf16[64,32,3,3,3]{0,1,4,3,2:T(8,128)(2,1)} %param.6) | copy-start | bytes 331780
  7.2 11.4 %copy-start.3 = (pred[8,10]{0,1:T(8,128)(4,1)S(1)}, pred[8,10]{0,1:T(8,128)(4,1)}, u32[]{:S(2)}) copy-start(pred[8,10]{0,1:T(8,128)(4,1)} %constant.19) | copy-start | bytes 244
  7.2 59.9 %all-to-all-start = ((bf16[32,16,2,1024]{3,2,1,0:T(2,128)(2,1)}), bf16[32,16,2,1024]{3,2,1,0:T(2,128)(2,1)S(1)}, u32[]{:S(2)}, u32[]{:S(2)}) async-start(bf16[32,16,2,1024]{3,2,1,0:T(2,128)(2,1)} %param.4), calls=%async_computation | async-start | bytes 4194304 | tf_op jit(solution)/shard_map/all_to_all | solution.py:63
  16.9 275.2 %all-reduce.3.cloned.1.call-start = ((), (), s32[]{:S(2)}) async-start(), calls=%async_computation.1 | async-start | bytes 884736 | tf_op jit(solution)/shard_map/psum | solution.py:12
  79.3 36.3 %copy-start.4 = (pred[8,9]{0,1:T(8,128)(4,1)S(1)}, pred[8,9]{0,1:T(8,128)(4,1)}, u32[]{:S(2)}) copy-start(pred[8,9]{0,1:T(8,128)(4,1)} %constant.17) | copy-start | bytes 220
  79.3 36.3 %copy-start.5 = (bf16[32,16,3,3,3]{0,1,4,3,2:T(8,128)(2,1)S(1)}, bf16[32,16,3,3,3]{0,1,4,3,2:T(8,128)(2,1)}, u32[]{:S(2)}) copy-start(bf16[32,16,3,3,3]{0,1,4,3,2:T(8,128)(2,1)} %param.5) | copy-start | bytes 82948
  138.3 3.1 copy-start.2
  154.5 310.0 %all-reduce.5.cloned.1.call-start = ((), (), s32[]{:S(2)}) async-start(), calls=%async_computation.2 | async-start | bytes 884736 | tf_op jit(solution)/shard_map/psum | solution.py:13
  202.7 89.3 %copy-start.1 = (bf16[32,4,1,8,8,32]{5,3,4,1,0,2:T(8,128)(2,1)S(1)}, bf16[32,4,1,8,8,32]{5,3,4,1,0,2:T(8,128)(2,1)}, u32[]{:S(2)}) copy-start(bf16[32,4,1,8,8,32]{5,3,4,1,0,2:T(8,128)(2,1)} %copy.66) | copy-start | bytes 1572868
Sparse Core Ops, SparseCore 0:
  154.7 63.2 all-reduce.2
  292.3 144.7 all-reduce.4
